TPU v7x, 512 devices: a whole 4x4x16 slice. The times are simulated.
512 devices in a mesh: expert: 32 (over z_hi, x, core), row: 4 (over z_lo), col: 4 (over y).
Axes of the slice: x: 4, y: 4, z: 16 (z_hi: 4, z_lo: 4; z = z_hi * 4 + z_lo), core: 2. Of those that a mesh axis runs over, the one named last changes fastest.
Arguments:
- tokens: bfloat16 [32768, 3584], P(('expert', 'col'), 'row'), may hold values from -6 to 6
- slots: int32 [128, 6, 32, 2], P(('expert', 'col')), may hold values from 0 to 255
- counts: int32 [6, 32], replicated, may hold values from 1 to 256, as said below
- owner: int32 [32], replicated, may hold values from 0 to 31, each once
Outputs:
- moments: float32 [32, 3584, 3584], P('expert', 'row', 'col')
Inputs may be any that keep to these rules, and one draw needn't show every extreme that they name: `counts`: in every panel at least one expert's count is 256.
All inputs are finite; a program needn't handle non-finite values.
Results may differ from a plain program's by a relative error of at most 0.0003.
Values may be sent and summed in bfloat16 or wider, within the bound.
No kernel may reach another device: no remote copies, remote signals or barrier semaphores. Data moves between devices by JAX's collectives and lax.ppermute only.
A program may use at most 64 MiB of HBM per device.

v0:
```python
import jax
import jax.numpy as jnp
from jax import lax
from jax.sharding import PartitionSpec as P


def from_root(value, axis, root):
    mine = lax.axis_index(axis) == root
    return lax.psum(jnp.where(mine, value, jnp.zeros_like(value)), axis)


def panel_moment(outgoing):
    received = lax.all_to_all(outgoing, "expert", split_axis=1, concat_axis=1, tiled=True)
    panel_count = received.shape[0]
    feature_count = received.shape[3]
    left_rows = lax.all_gather(received, "col", axis=2, tiled=True)
    left_rows = left_rows.reshape(panel_count, -1, feature_count)
    right_rows = from_root(left_rows, "row", lax.axis_index("col"))
    return jnp.einsum("kpa,kpb->ab", left_rows, right_rows, preferred_element_type=jnp.float32)


def per_device(tokens, slots, counts, owner):
    col_count = lax.axis_size("col")
    slot_count = slots.shape[3]
    block_index = lax.axis_index("expert") * col_count + lax.axis_index("col")
    inverse = jnp.argsort(owner)
    dest_slots = jnp.take(slots[0], inverse, axis=1)
    dest_counts = jnp.take(counts, inverse, axis=1)
    position = block_index * slot_count + jnp.arange(slot_count, dtype=jnp.int32)
    usable = position[None, None, :] < dest_counts[:, :, None]
    picked = tokens[dest_slots]
    outgoing = jnp.where(usable[..., None], picked, jnp.zeros_like(picked))
    own_expert = inverse[lax.axis_index("expert")]
    row_total = jnp.sum(jnp.take(counts, own_expert, axis=1)).astype(jnp.float32)
    moment_tile = jnp.zeros((tokens.shape[1], tokens.shape[1]), jnp.float32)
    for panel in range(outgoing.shape[0]):
        moment_tile = moment_tile + panel_moment(outgoing[panel : panel + 1])
    return (moment_tile / row_total)[None]


def solution(mesh):
    return jax.shard_map(
        per_device,
        mesh=mesh,
        in_specs=(P(("expert", "col"), "row"), P(("expert", "col"), None, None, None), P(), P()),
        out_specs=P("expert", "row", "col"),
        check_vma=False,
    )
```

profile of v0, /device:TPU:1, one launch (start us, length us, event | category | flops | bytes accessed | tf_op | source)
XLA Modules:
  0.0 362.5 jit_solution(1238533840400708526)
XLA Ops:
  6.5 0.0 copy-start
  6.5 2.3 sort.17
  8.9 0.8 copy.21
  9.7 0.8 copy.22
  10.5 0.6 gather_fusion
  11.0 0.6 gather_fusion.1
  11.6 0.1 select_bitcast_fusion.6
  11.7 0.1 compare_select_fusion
  11.8 0.4 copy.23
  12.2 0.1 reshape.248
  12.3 0.0 copy-done
  12.3 2.3 gather_fusion.2
  14.6 0.3 reshape.247
  14.9 0.1 broadcast_compare_fusion
  15.0 0.8 broadcast_select_fusion
  15.8 1.2 fusion.17
  17.0 35.4 %all_to_all.30 = bf16[1,32,2,896]{3,2,0,1:T(2,128)(2,1)S(1)} all-to-all(bf16[1,32,2,896]{3,2,0,1:T(2,128)(2,1)S(1)} %get-tuple-element.25), channel_id=1, replica_groups=mesh['expert'=32,'row'=4,'col'=4] {'expert'}, dimensions={1} | all-to-all | bytes 229376 | tf_op jit(solution)/shard_map/all_to_all | solution.py:13
  52.4 20.9 %all_to_all.31 = bf16[1,32,2,896]{3,2,0,1:T(2,128)(2,1)S(1)} all-to-all(bf16[1,32,2,896]{3,2,0,1:T(2,128)(2,1)S(1)} %get-tuple-element.26), channel_id=1, replica_groups=mesh['expert'=32,'row'=4,'col'=4] {'expert'}, dimensions={1} | all-to-all | bytes 229376 | tf_op jit(solution)/shard_map/all_to_all | solution.py:13
  73.3 20.9 %all_to_all.32 = bf16[1,32,2,896]{3,2,0,1:T(2,128)(2,1)S(1)} all-to-all(bf16[1,32,2,896]{3,2,0,1:T(2,128)(2,1)S(1)} %get-tuple-element.28), channel_id=1, replica_groups=mesh['expert'=32,'row'=4,'col'=4] {'expert'}, dimensions={1} | all-to-all | bytes 229376 | tf_op jit(solution)/shard_map/all_to_all | solution.py:13
  94.3 20.9 %all_to_all.33 = bf16[1,32,2,896]{3,2,0,1:T(2,128)(2,1)S(1)} all-to-all(bf16[1,32,2,896]{3,2,0,1:T(2,128)(2,1)S(1)} %get-tuple-element.29), channel_id=1, replica_groups=mesh['expert'=32,'row'=4,'col'=4] {'expert'}, dimensions={1} | all-to-all | bytes 229376 | tf_op jit(solution)/shard_map/all_to_all | solution.py:13
  115.2 5.1 %all-to-all-start.2 = ((bf16[1,32,2,896]{3,2,0,1:T(2,128)(2,1)}), bf16[1,32,2,896]{3,2,0,1:T(2,128)(2,1)S(1)}, u32[]{:S(2)}, u32[]{:S(2)}) async-start(bf16[1,32,2,896]{3,2,0,1:T(2,128)(2,1)} %get-tuple-element.27), calls=%async_computation.2 | async-start | bytes 229376 | tf_op jit(solution)/shard_map/all_to_all | solution.py:13
  120.4 11.2 %all_gather.18 = bf16[1,32,8,896]{3,1,0,2:T(8,128)(2,1)S(1)} all-gather(bf16[1,32,2,896]{3,1,0,2:T(8,128)(2,1)S(1)} %copy.25), channel_id=1, replica_groups=mesh['expert'=32,'row'=4,'col'=4] {'col'}, dimensions={2}, use_global_device_ids=true | all-gather | bytes 573440 | tf_op jit(solution)/shard_map/all_gather | solution.py:16
  131.6 10.0 %all_gather.19 = bf16[1,32,8,896]{3,1,0,2:T(8,128)(2,1)S(1)} all-gather(bf16[1,32,2,896]{3,1,0,2:T(8,128)(2,1)S(1)} %copy.28), channel_id=1, replica_groups=mesh['expert'=32,'row'=4,'col'=4] {'col'}, dimensions={2}, use_global_device_ids=true | all-gather | bytes 573440 | tf_op jit(solution)/shard_map/all_gather | solution.py:16
  141.7 0.0 all-to-all-done.2
  141.7 19.5 %all-to-all-start.5 = ((bf16[1,32,2,896]{3,2,0,1:T(2,128)(2,1)}), bf16[1,32,2,896]{3,2,0,1:T(2,128)(2,1)S(1)}, u32[]{:S(2)}, u32[]{:S(2)}) async-start(bf16[1,32,2,896]{3,2,0,1:T(2,128)(2,1)} %get-tuple-element.24), calls=%async_computation.5 | async-start | bytes 229376 | tf_op jit(solution)/shard_map/all_to_all | solution.py:13
  161.2 0.0 all-reduce.3.cloned.1.call-start
  161.2 10.8 %all_gather.20 = bf16[1,32,8,896]{3,1,0,2:T(8,128)(2,1)S(1)} all-gather(bf16[1,32,2,896]{3,1,0,2:T(8,128)(2,1)S(1)} %copy.31), channel_id=1, replica_groups=mesh['expert'=32,'row'=4,'col'=4] {'col'}, dimensions={2}, use_global_device_ids=true | all-gather | bytes 573440 | tf_op jit(solution)/shard_map/all_gather | solution.py:16
  172.1 10.0 %all_gather.21 = bf16[1,32,8,896]{3,1,0,2:T(8,128)(2,1)S(1)} all-gather(bf16[1,32,2,896]{3,1,0,2:T(8,128)(2,1)S(1)} %copy.34), channel_id=1, replica_groups=mesh['expert'=32,'row'=4,'col'=4] {'col'}, dimensions={2}, use_global_device_ids=true | all-gather | bytes 573440 | tf_op jit(solution)/shard_map/all_gather | solution.py:16
  182.1 10.6 %all_gather.22 = bf16[1,32,8,896]{3,1,0,2:T(8,128)(2,1)S(1)} all-gather(bf16[1,32,2,896]{3,1,0,2:T(8,128)(2,1)S(1)} %copy.37), channel_id=1, replica_groups=mesh['expert'=32,'row'=4,'col'=4] {'col'}, dimensions={2}, use_global_device_ids=true | all-gather | bytes 573440 | tf_op jit(solution)/shard_map/all_gather | solution.py:16
  192.7 0.0 all-to-all-done.5
  192.7 10.8 %all_gather.23 = bf16[1,32,8,896]{3,1,0,2:T(8,128)(2,1)S(1)} all-gather(bf16[1,32,2,896]{3,1,0,2:T(8,128)(2,1)S(1)} %copy.40), channel_id=1, replica_groups=mesh['expert'=32,'row'=4,'col'=4] {'col'}, dimensions={2}, use_global_device_ids=true | all-gather | bytes 573440 | tf_op jit(solution)/shard_map/all_gather | solution.py:16
  203.6 1.0 select_bitcast_fusion
  204.5 0.9 select_bitcast_fusion.1
  205.5 0.0 copy-start.6
  205.5 1.0 select_bitcast_fusion.2
  206.4 0.9 select_bitcast_fusion.3
  207.3 0.9 select_bitcast_fusion.4
  208.3 1.0 select_bitcast_fusion.5
  209.2 0.0 all-reduce.3.cloned.1.call-update
  209.3 0.6 dynamic_slice.3
  211.8 0.0 copy-done.6
  211.8 0.7 select_reduce_fusion
  213.2 135.0 %all-reduce.3.cloned.1.call-done = (bf16[256,896]{1,0:T(8,128)(2,1)}, bf16[256,896]{1,0:T(8,128)(2,1)}, bf16[256,896]{1,0:T(8,128)(2,1)}, bf16[256,896]{1,0:T(8,...) async-done(((bf16[256,896]{1,0:T(8,128)(2,1)}, bf16[256,896]{1,0:T(8,128)(2,1)}, bf16[256,896]{1,0:T(8,128)(2,1)}, bf16[256,896]{1,0:T(8,128)(2,1)}, ...) | async-done | bytes 2752528 | tf_op jit(solution)/shard_map/psum | solution.py:9
  348.1 0.0 copy-start.5
  348.1 0.0 copy-start.4
  348.1 1.8 fusion.1
  349.9 0.0 copy-done.5
  349.9 0.0 copy-start.3
  349.9 0.7 fusion.3
  350.6 0.0 copy-done.4
  350.6 0.0 copy-start.2
  350.6 0.7 fusion.5
  351.3 0.0 copy-done.3
  351.3 0.0 copy-start.1
  351.3 0.7 fusion.9
  352.0 0.0 copy-done.2
  352.0 0.7 fusion.7
  352.7 0.0 copy-done.1
  352.7 2.9 divide_bitcast_fusion
  (12 shorter events, 0.1 us)
Async XLA Ops:
  6.5 5.8 %copy-start = (bf16[256,896]{1,0:T(8,128)(2,1)S(1)}, bf16[256,896]{1,0:T(8,128)(2,1)}, u32[]{:S(2)}) copy-start(bf16[256,896]{1,0:T(8,128)(2,1)} %param.4) | copy-start | bytes 1376260
  115.2 26.5 %all-to-all-start.2 = ((bf16[1,32,2,896]{3,2,0,1:T(2,128)(2,1)}), bf16[1,32,2,896]{3,2,0,1:T(2,128)(2,1)S(1)}, u32[]{:S(2)}, u32[]{:S(2)}) async-start(bf16[1,32,2,896]{3,2,0,1:T(2,128)(2,1)} %get-tuple-element.27), calls=%async_computation.2 | async-start | bytes 229376 | tf_op jit(solution)/shard_map/all_to_all | solution.py:13
  141.7 51.0 %all-to-all-start.5 = ((bf16[1,32,2,896]{3,2,0,1:T(2,128)(2,1)}), bf16[1,32,2,896]{3,2,0,1:T(2,128)(2,1)S(1)}, u32[]{:S(2)}, u32[]{:S(2)}) async-start(bf16[1,32,2,896]{3,2,0,1:T(2,128)(2,1)} %get-tuple-element.24), calls=%async_computation.5 | async-start | bytes 229376 | tf_op jit(solution)/shard_map/all_to_all | solution.py:13
  161.2 187.0 %all-reduce.3.cloned.1.call-start = ((), (), s32[]{:S(2)}) async-start(), calls=%async_computation.6 | async-start | bytes 5505024 | tf_op jit(solution)/shard_map/psum | solution.py:9
  205.5 6.3 %copy-start.6 = (s32[6,32]{1,0:T(8,128)S(1)}, s32[6,32]{1,0:T(8,128)}, u32[]{:S(2)}) copy-start(s32[6,32]{1,0:T(8,128)} %param.6) | copy-start | bytes 2308
  348.1 1.8 copy-start.5
  348.1 2.5 copy-start.4
  349.9 1.4 copy-start.3
  350.6 1.4 copy-start.2
  351.3 1.4 copy-start.1
Sparse Core Ops, SparseCore 0:
  209.4 138.7 all-reduce.2
where the time goes:
time: 363 us
  blocking collectives  162 us (45%)
  waiting for transfers between devices  135 us (37%)
  starting transfers between devices  24.6 us (7%)
  between operations  16.2 us (4%)
  other arithmetic  9.83 us (3%)
  local copies, waits for them, and re-layouts  7.67 us (2%)
  matrix products  7.42 us (2%)
    psum x1, waiting for transfers between devices, from_root(): return lax.psum(jnp.where(mine, value, jnp.zeros_like(value)), axis)  135 us
    all_to_all x4, blocking collectives, panel_moment(): lax.all_to_all(outgoing, 'expert', split_axis=1, concat_axis=1, tiled=True)  98.2 us
    all_gather x6, blocking collectives, panel_moment(): left_rows = lax.all_gather(received, 'col', axis=2, tiled=True)  63.5 us
    all_to_all x2, starting transfers between devices, panel_moment(): lax.all_to_all(outgoing, 'expert', split_axis=1, concat_axis=1, tiled=True)  24.6 us
    dot_general x6, matrix products, panel_moment(): jnp.einsum('kpa,kpb->ab', left_rows, right_rows, preferred_element_type=j...  7.42 us
  transfers between devices with their start and end apart: 3, of which 1 were waited for; matrix products, arithmetic and copies ran while one was open for 0% of the time, Pallas kernels for 0%

commit v1 on v0

--- a/solution.py
+++ b/solution.py
@@ -13,7 +13,9 @@
     received = lax.all_to_all(outgoing, "expert", split_axis=1, concat_axis=1, tiled=True)
     panel_count = received.shape[0]
     feature_count = received.shape[3]
-    left_rows = lax.all_gather(received, "col", axis=2, tiled=True)
+    left_rows = jnp.concatenate(
+        lax.all_to_all(jnp.stack([received] * lax.axis_size("col")), "col", 0, 0), axis=2
+    )
     left_rows = left_rows.reshape(panel_count, -1, feature_count)
     right_rows = from_root(left_rows, "row", lax.axis_index("col"))
     return jnp.einsum("kpa,kpb->ab", left_rows, right_rows, preferred_element_type=jnp.float32)

time: 363 us -> 382 us (1.052)
  local copies, waits for them, and re-layouts: 7.67 us -> 38.3 us
  blocking collectives: 162 us -> 180 us
  starting transfers between devices: 24.6 us -> 7.15 us
  waiting for transfers between devices: 135 us -> 123 us
    all_gather x6 -> x0, blocking collectives: 63.5 us -> none  [panel_moment(): left_rows = lax.all_gather(received, 'col', axis=2, tiled=True)]
    all_to_all x4 -> x6, blocking collectives: 98.2 us -> 140 us  [panel_moment(): lax.all_to_all(outgoing, 'expert', split_axis=1, concat_axis=1, tiled=True)]
    all_to_all x0 -> x4, blocking collectives: none -> 39.8 us  [panel_moment(): lax.all_to_all(jnp.stack([received] * lax.axis_size('col')), 'col', 0, 0)]
    another operation x0 -> x18, local copies, waits for them, and re-layouts: none -> 19.1 us
    psum x1, waiting for transfers between devices: 135 us -> 116 us  [from_root(): return lax.psum(jnp.where(mine, value, jnp.zeros_like(value)), axis)]
    all_to_all x2, starting transfers between devices: 24.6 us -> 6.93 us  [panel_moment(): lax.all_to_all(jnp.stack([received] * lax.axis_size('col')), 'col', 0, 0)]
    select_n x0 -> x6, local copies, waits for them, and re-layouts: none -> 9.62 us  [from_root(): return lax.psum(jnp.where(mine, value, jnp.zeros_like(value)), axis)]
    all_to_all x2, waiting for transfers between devices: 0.01 us -> 6.54 us  [panel_moment(): lax.all_to_all(jnp.stack([received] * lax.axis_size('col')), 'col', 0, 0)]
  transfers between devices with their start and end apart: 3 -> 3, of which waited for: 1 -> 2; matrix products, arithmetic and copies ran while one was open for 0% -> 6% of each run, Pallas kernels for 0% -> 0%
where the time goes in v1:
time: 382 us; the launch traced here: 380 us
  blocking collectives  180 us (47%)
  waiting for transfers between devices  123 us (32%)
  local copies, waits for them, and re-layouts  38.3 us (10%)
  between operations  16.3 us (4%)
  other arithmetic  8.69 us (2%)
  matrix products  7.28 us (2%)
  starting transfers between devices  7.15 us (2%)
    all_to_all x6, blocking collectives, panel_moment(): lax.all_to_all(outgoing, 'expert', split_axis=1, concat_axis=1, tiled=True)  140 us
    psum x1, waiting for transfers between devices, from_root(): return lax.psum(jnp.where(mine, value, jnp.zeros_like(value)), axis)  116 us
    all_to_all x4, blocking collectives, panel_moment(): lax.all_to_all(jnp.stack([received] * lax.axis_size('col')), 'col', 0, 0)  39.8 us
    another operation x12, local copies, waits for them, and re-layouts  16.2 us
    select_n x6, local copies, waits for them, and re-layouts, from_root(): return lax.psum(jnp.where(mine, value, jnp.zeros_like(value)), axis)  9.62 us
  transfers between devices with their start and end apart: 3, of which 2 were waited for; matrix products, arithmetic and copies ran while one was open for 6% of the time, Pallas kernels for 0%

profile of v1, /device:TPU:1, one launch (start us, length us, event | category | flops | bytes accessed | tf_op | source)
XLA Modules:
  0.0 380.4 jit_solution(13951806302432291816)
XLA Ops:
  6.5 2.3 sort.17
  8.9 0.8 copy.11
  9.7 0.8 copy.12
  10.5 0.6 gather_fusion
  11.0 0.6 gather_fusion.1
  11.8 0.4 copy.13
  12.3 2.3 gather_fusion.2
  14.6 0.3 reshape.283
  15.0 0.8 broadcast_select_fusion
  15.8 0.5 fusion
  16.3 35.4 %all_to_all.78 = bf16[1,32,2,896]{3,2,0,1:T(2,128)(2,1)S(1)} all-to-all(bf16[1,32,2,896]{3,2,0,1:T(2,128)(2,1)S(1)} %get-tuple-element.24), channel_id=1, replica_groups=mesh['expert'=32,'row'=4,'col'=4] {'expert'}, dimensions={1} | all-to-all | bytes 229376 | tf_op jit(solution)/shard_map/all_to_all | solution.py:13
  51.8 20.9 %all_to_all.79 = bf16[1,32,2,896]{3,2,0,1:T(2,128)(2,1)S(1)} all-to-all(bf16[1,32,2,896]{3,2,0,1:T(2,128)(2,1)S(1)} %get-tuple-element.25), channel_id=1, replica_groups=mesh['expert'=32,'row'=4,'col'=4] {'expert'}, dimensions={1} | all-to-all | bytes 229376 | tf_op jit(solution)/shard_map/all_to_all | solution.py:13
  72.7 20.9 %all_to_all.80 = bf16[1,32,2,896]{3,2,0,1:T(2,128)(2,1)S(1)} all-to-all(bf16[1,32,2,896]{3,2,0,1:T(2,128)(2,1)S(1)} %get-tuple-element.26), channel_id=1, replica_groups=mesh['expert'=32,'row'=4,'col'=4] {'expert'}, dimensions={1} | all-to-all | bytes 229376 | tf_op jit(solution)/shard_map/all_to_all | solution.py:13
  93.6 20.9 %all_to_all.81 = bf16[1,32,2,896]{3,2,0,1:T(2,128)(2,1)S(1)} all-to-all(bf16[1,32,2,896]{3,2,0,1:T(2,128)(2,1)S(1)} %get-tuple-element.27), channel_id=1, replica_groups=mesh['expert'=32,'row'=4,'col'=4] {'expert'}, dimensions={1} | all-to-all | bytes 229376 | tf_op jit(solution)/shard_map/all_to_all | solution.py:13
  114.5 20.9 %all_to_all.82 = bf16[1,32,2,896]{3,2,0,1:T(2,128)(2,1)S(1)} all-to-all(bf16[1,32,2,896]{3,2,0,1:T(2,128)(2,1)S(1)} %get-tuple-element.28), channel_id=1, replica_groups=mesh['expert'=32,'row'=4,'col'=4] {'expert'}, dimensions={1} | all-to-all | bytes 229376 | tf_op jit(solution)/shard_map/all_to_all | solution.py:13
  135.5 20.9 %all_to_all.83 = bf16[1,32,2,896]{3,2,0,1:T(2,128)(2,1)S(1)} all-to-all(bf16[1,32,2,896]{3,2,0,1:T(2,128)(2,1)S(1)} %get-tuple-element.29), channel_id=1, replica_groups=mesh['expert'=32,'row'=4,'col'=4] {'expert'}, dimensions={1} | all-to-all | bytes 229376 | tf_op jit(solution)/shard_map/all_to_all | solution.py:13
  156.4 0.2 stack.12
  156.6 12.2 %all_to_all.84 = bf16[4,1,32,2,896]{4,3,2,1,0:T(2,128)(2,1)S(1)} all-to-all(bf16[4,1,32,2,896]{4,3,2,1,0:T(2,128)(2,1)S(1)} %stack.12), channel_id=1, replica_groups=mesh['expert'=32,'row'=4,'col'=4] {'col'}, dimensions={0} | all-to-all | bytes 917504 | tf_op jit(solution)/shard_map/all_to_all | solution.py:17
  168.8 0.2 stack.13
  169.0 9.7 %all_to_all.85 = bf16[4,1,32,2,896]{4,3,2,1,0:T(2,128)(2,1)S(1)} all-to-all(bf16[4,1,32,2,896]{4,3,2,1,0:T(2,128)(2,1)S(1)} %stack.13), channel_id=1, replica_groups=mesh['expert'=32,'row'=4,'col'=4] {'col'}, dimensions={0} | all-to-all | bytes 917504 | tf_op jit(solution)/shard_map/all_to_all | solution.py:17
  178.7 0.2 stack.14
  179.0 9.0 %all_to_all.86 = bf16[4,1,32,2,896]{4,3,2,1,0:T(2,128)(2,1)S(1)} all-to-all(bf16[4,1,32,2,896]{4,3,2,1,0:T(2,128)(2,1)S(1)} %stack.14), channel_id=1, replica_groups=mesh['expert'=32,'row'=4,'col'=4] {'col'}, dimensions={0} | all-to-all | bytes 917504 | tf_op jit(solution)/shard_map/all_to_all | solution.py:17
  187.9 0.2 stack.16
  188.2 9.0 %all_to_all.87 = bf16[4,1,32,2,896]{4,3,2,1,0:T(2,128)(2,1)S(1)} all-to-all(bf16[4,1,32,2,896]{4,3,2,1,0:T(2,128)(2,1)S(1)} %stack.16), channel_id=1, replica_groups=mesh['expert'=32,'row'=4,'col'=4] {'col'}, dimensions={0} | all-to-all | bytes 917504 | tf_op jit(solution)/shard_map/all_to_all | solution.py:17
  197.1 1.0 stack.17
  198.1 3.5 all-to-all-start.11
  201.6 6.5 %all-to-all-done.11 = bf16[4,1,32,2,896]{4,3,2,1,0:T(2,128)(2,1)S(1)} async-done(((bf16[4,1,32,2,896]{4,3,2,1,0:T(2,128)(2,1)}), bf16[4,1,32,2,896]{4,3,2,1,0:T(2,128)(2,1)S(1)}, u32[]{:S(2)}, u32[]{:S(2)}) %all-to-all-start.11) | async-done | bytes 458784 | tf_op jit(solution)/shard_map/all_to_all | solution.py:17
  208.2 1.0 stack.15
  209.2 3.5 all-to-all-start.7
  212.6 0.2 all-reduce.3.cloned.1.call-start
  212.9 1.5 broadcast_select_fusion.1
  214.4 1.1 copy.26
  215.5 2.0 reshape.225
  217.4 2.1 copy.24
  219.5 2.0 reshape.222
  221.5 1.5 broadcast_select_fusion.5
  223.0 1.1 copy.18
  224.1 2.0 reshape.213
  226.1 1.5 broadcast_select_fusion.3
  227.6 1.1 copy.22
  228.7 2.0 reshape.219
  230.7 2.1 copy.20
  232.8 2.0 reshape.216
  234.8 2.1 copy.16
  236.9 2.0 reshape.210
  238.9 0.6 dynamic_slice.3
  241.4 0.7 select_reduce_fusion
  242.8 1.1 copy.25
  243.8 2.0 reshape.224
  245.8 0.3 copy.23
  246.1 0.9 reshape.221
  247.1 0.3 copy.21
  247.4 0.2 reshape.218
  247.6 0.3 copy.19
  247.9 1.0 reshape.215
  248.9 0.3 copy.17
  249.4 0.3 copy.15
  249.9 116.3 %all-reduce.3.cloned.1.call-done = (bf16[256,896]{1,0:T(8,128)(2,1)}, bf16[256,896]{1,0:T(8,128)(2,1)}, bf16[256,896]{1,0:T(8,128)(2,1)}, bf16[256,896]{1,0:T(8,...) async-done(((bf16[256,896]{1,0:T(8,128)(2,1)}, bf16[256,896]{1,0:T(8,128)(2,1)}, bf16[256,896]{1,0:T(8,128)(2,1)}, bf16[256,896]{1,0:T(8,128)(2,1)}, ...) | async-done | bytes 2752528 | tf_op jit(solution)/shard_map/psum | solution.py:9
  366.2 1.8 fusion.5
  368.0 0.7 fusion.4
  368.7 0.7 fusion.3
  369.4 0.7 fusion.1
  370.1 0.7 fusion.2
  370.8 2.8 divide_bitcast_fusion
  (34 shorter events, 0.9 us)
Async XLA Ops:
  6.5 5.8 %copy-start = (bf16[256,896]{1,0:T(8,128)(2,1)S(1)}, bf16[256,896]{1,0:T(8,128)(2,1)}, u32[]{:S(2)}) copy-start(bf16[256,896]{1,0:T(8,128)(2,1)} %param.4) | copy-start | bytes 1376260
  198.1 10.0 %all-to-all-start.11 = ((bf16[4,1,32,2,896]{4,3,2,1,0:T(2,128)(2,1)}), bf16[4,1,32,2,896]{4,3,2,1,0:T(2,128)(2,1)S(1)}, u32[]{:S(2)}, u32[]{:S(2)}) async-start(bf16[4,1,32,2,896]{4,3,2,1,0:T(2,128)(2,1)} %stack.17), calls=%async_computation.11 | async-start | bytes 917504 | tf_op jit(solution)/shard_map/all_to_all | solution.py:17
  209.2 16.9 %all-to-all-start.7 = ((bf16[4,1,32,2,896]{4,3,2,1,0:T(2,128)(2,1)}), bf16[4,1,32,2,896]{4,3,2,1,0:T(2,128)(2,1)S(1)}, u32[]{:S(2)}, u32[]{:S(2)}) async-start(bf16[4,1,32,2,896]{4,3,2,1,0:T(2,128)(2,1)} %stack.15), calls=%async_computation.7 | async-start | bytes 917504 | tf_op jit(solution)/shard_map/all_to_all | solution.py:17
  212.6 153.5 %all-reduce.3.cloned.1.call-start = ((), (), s32[]{:S(2)}) async-start(), calls=%async_computation.12 | async-start | bytes 5505024 | tf_op jit(solution)/shard_map/psum | solution.py:9
  230.7 10.7 %copy-start.9 = (s32[6,32]{1,0:T(8,128)S(1)}, s32[6,32]{1,0:T(8,128)}, u32[]{:S(2)}) copy-start(s32[6,32]{1,0:T(8,128)} %param.6) | copy-start | bytes 2308
  247.4 118.8 %copy-start.2 = (bf16[256,896]{1,0:T(8,128)(2,1)S(1)}, bf16[256,896]{1,0:T(8,128)(2,1)}, u32[]{:S(2)}) copy-start(bf16[256,896]{1,0:T(8,128)(2,1)} %reshape.221) | copy-start | bytes 1376260
  366.2 1.8 copy-start.8
  366.2 2.5 copy-start.3
  366.2 2.5 copy-start.7
  368.0 1.4 copy-start.6
  368.7 1.4 copy-start.5
  369.4 1.4 copy-start.1
  369.4 1.4 copy-start.4
Sparse Core Ops, SparseCore 0:
  239.0 127.1 all-reduce.2
